TPU v7x, 32 devices: a whole 2x2x4 slice. The times are simulated.
32 devices in a mesh: row: 8 (over z, y), col: 4 (over x, core).
Axes of the slice: x: 2, y: 2, z: 4, core: 2. Of those that a mesh axis runs over, the one named last changes fastest.
Arguments:
- amplitudes: bfloat16 [16384, 1024], P('col', 'row'), may hold values from -6 to 6
- integrals: bfloat16 [256, 64, 8192], P('row', None, 'col'), may hold values from -0.125 to 0.125
- slot_tiles: int32 [256, 128], P('row', 'col'), may hold values from 0 to 63, as said below
- tile_count: int32 [256, 4], P('row', 'col'), may hold values from 1 to 32, as said below
- denominator: float32 [16384, 1024], P(('row', 'col')), may hold values from 1 to 4
Outputs:
- update: bfloat16 [16384, 1024], P(('row', 'col'))
Inputs may be any that keep to these rules, and one draw needn't show every extreme that they name: `slot_tiles`: within one residual tile and one column block, the 32 slots name distinct tiles. `tile_count`: in every column block some residual tile has all 32 slots live.
All inputs are finite; a program needn't handle non-finite values.
Results may differ from a plain program's by a relative error of at most 0.014.
Values may be sent and summed in bfloat16 or wider, within the bound.
A program may use at most 192 MiB of HBM per device.

v0:
```python
import functools

import jax
import jax.numpy as jnp
from jax import lax
from jax.experimental import pallas as pl
from jax.experimental.pallas import tpu as pltpu
from jax.sharding import PartitionSpec as P

LANES = 128
PIECES = 2


def line_order(size, at):
    return sorted(range(size), key=lambda k: (abs(k - at), -min(k, size - 1 - k)))


def kernel(
    dims, slots_ref, count_ref, amp_ref, ints_ref, den_ref, out_ref,
    panel, tiles, dense, partial, landed, den, table, table_ref,
    load_sem, ints_sem, send_sem, recv_sem, part_send_sem, part_recv_sem,
):
    n_row, n_col, na, nb = dims
    tile_rows = ints_ref.shape[0]
    tile_size = ints_ref.shape[1]
    depth, pairs = amp_ref.shape
    groups = ints_ref.shape[2] // LANES
    quarter = partial.shape[1] // n_col
    row, col = lax.axis_index("row"), lax.axis_index("col")
    pos, side = row // nb, row % nb

    def device(a, b):
        return {"row": a * nb + b}

    up, down, across = device(pos + 1, side), device(pos - 1, side), device(pos, 1 - side)
    has_up, has_down = pos < na - 1, pos > 0

    barrier = pltpu.get_barrier_semaphore()

    @pl.when(has_up)
    def _():
        pl.semaphore_signal(barrier, inc=1, device_id=up)

    @pl.when(has_down)
    def _():
        pl.semaphore_signal(barrier, inc=1, device_id=down)

    pl.semaphore_signal(barrier, inc=1, device_id=across)
    for k in range(1, n_col):
        pl.semaphore_signal(barrier, inc=1, device_id={"col": lax.rem(col + k, n_col)})
    pl.semaphore_wait(barrier, n_col + has_up.astype(jnp.int32) + has_down.astype(jnp.int32))

    def order(t):
        value = jnp.int32(0)
        for k in range(na):
            for i, which in enumerate(line_order(na, k)):
                value = value + jnp.where((pos == k) & (t == i), which, 0)
        return value

    def mine(t):
        return order(t) * nb + side

    def other(t):
        return order(t) * nb + 1 - side

    def hop(source, j, h, way):
        to = (up, down, across)[way]
        return pltpu.make_async_remote_copy(
            source, panel.at[j, h], send_sem.at[j, h, way], recv_sem.at[j, h], device_id=to
        )

    def each_hop(t, own, h, act):
        a = order(t)
        goes_up, goes_down = has_up & (a <= pos), has_down & (a >= pos)
        if not own and h < PIECES // 2:
            return
        if not own:
            goes_up, goes_down = goes_up & (a == 0), goes_down & (a == na - 1)
        pl.when(goes_up)(lambda: act(0))
        pl.when(goes_down)(lambda: act(1))
        if own and h < PIECES // 2:
            act(2)
        elif own:
            pl.when((a == pos) | ((a > 0) & (a < na - 1)))(lambda: act(2))

    def piece(h):
        return pl.ds(h * (depth // PIECES), depth // PIECES)

    def pass_on(t, own, h):
        j = mine(t) if own else other(t)
        hop(panel.at[j, h], j, h, 2).wait_recv()
        each_hop(t, own, h, lambda way: hop(panel.at[j, h], j, h, way).start())

    for h in range(PIECES):
        each_hop(jnp.int32(0), True, h, lambda way: hop(amp_ref.at[piece(h)], row, h, way).start())

    load_own = [
        pltpu.make_async_copy(amp_ref.at[piece(h)], panel.at[row, h], load_sem.at[1 + h]) for h in range(PIECES)
    ]
    load_den = pltpu.make_async_copy(den_ref, den, load_sem.at[0])

    def load_ints(p):
        return pltpu.make_async_copy(
            ints_ref.at[:, :, pl.ds(p * LANES, LANES)],
            tiles.at[pl.ds(p * tile_rows, tile_rows)],
            ints_sem.at[p],
        )

    for p in range(groups):
        load_ints(p).start()
    for copy in load_own:
        copy.start()
    load_den.start()

    virtual = lax.broadcasted_iota(jnp.int32, table.shape, 1)
    residual = lax.broadcasted_iota(jnp.int32, table.shape, 0)
    slots, count = slots_ref[...], count_ref[...]
    found = jnp.full(table.shape, 2 * groups * tile_rows, jnp.int32)
    for s in range(slots.shape[1]):
        turned = jnp.where(virtual % 2 != s % 2, groups * tile_rows, 0)
        hit = (slots[:, s:s + 1] == virtual) & (count > s)
        found = jnp.where(hit, turned + (s // 2 * tile_rows) + residual, found)
    table[...] = found

    batch = 8 if tile_rows % 8 == 0 else 1
    swapped = groups * tile_rows
    for p in range(groups):
        load_ints(p).wait()

        @pl.loop(0, tile_rows // batch)
        def _(a):
            x = tiles[pl.ds(p * tile_rows + a * batch, batch)]
            tiles[pl.ds(swapped + p * tile_rows + a * batch, batch)] = jnp.concatenate(
                [x[:, :, LANES // 2:], x[:, :, : LANES // 2]], axis=2
            )

    tiles[2 * swapped] = jnp.zeros((tile_size, LANES), jnp.bfloat16)
    load_table = pltpu.make_async_copy(table, table_ref, load_sem.at[1 + PIECES])
    load_table.start()
    load_table.wait()
    first = lax.broadcasted_iota(jnp.int32, (tile_size, LANES), 1) < LANES // 2

    @pl.loop(0, tile_rows)
    def _(a):
        for g in range(depth // LANES):
            dense[pl.ds(pl.multiple_of(a * tile_size, tile_size), tile_size), g * LANES:(g + 1) * LANES] = jnp.where(
                first, tiles[table_ref[a, 2 * g]], tiles[table_ref[a, 2 * g + 1]]
            )

    for copy in load_own:
        copy.wait()
    load_den.wait()

    def target(k):
        chip = lax.rem(col // 2 + k // 2, n_col // 2)
        return chip * 2 + lax.rem(col + k, 2)

    def rows_of(k):
        return pl.ds(pl.multiple_of(target(k) * quarter, quarter), quarter)

    def part_copy(j, k):
        return pltpu.make_async_remote_copy(
            partial.at[j, rows_of(k)], landed.at[k - 1, j],
            part_send_sem.at[j, k - 1], part_recv_sem.at[j, k - 1], device_id={"col": target(k)},
        )

    def multiply(*blocks):
        @pl.loop(0, n_col)
        def _(i):
            k = n_col - 1 - i
            rows = rows_of(k)
            right = [panel[j].reshape(depth, pairs) for j in blocks]
            right = right[0] if len(right) == 1 else jnp.concatenate(right, axis=1)
            product = jnp.dot(dense[rows, :], right, preferred_element_type=jnp.float32).astype(jnp.bfloat16)
            for n, j in enumerate(blocks):
                partial[j, rows, :] = product[:, n * pairs:(n + 1) * pairs]

            @pl.when(k > 0)
            def _():
                for j in blocks:
                    part_copy(j, k).start()

    def finish(*blocks):
        for j in blocks:
            for k in range(1, n_col):
                part_copy(j, k).wait_recv()
            total = partial[j, rows_of(0), :].astype(jnp.float32)
            for k in range(1, n_col):
                total = total + landed[k - 1, j].astype(jnp.float32)
            columns = pl.ds(pl.multiple_of(j * pairs, pairs), pairs)
            out_ref[:, columns] = (total / den[:, columns]).astype(jnp.bfloat16)

    def pass_block(t, own):
        for h in reversed(range(PIECES)) if not own else range(PIECES):
            pass_on(t, own, h)

    inside = has_up & has_down
    pass_block(jnp.int32(1), True)
    pl.when(inside)(lambda: pass_block(jnp.int32(2), True))
    pass_block(jnp.int32(0), False)
    multiply(row)

    @pl.loop(1, na)
    def _(t):
        @pl.when(t > 1)
        def _():
            pl.when(jnp.logical_not(inside))(lambda: pass_block(t, True))
            pass_block(t - 1, False)
            pl.when(inside & (t < na - 1))(lambda: pass_block(t + 1, True))

        multiply(mine(t), other(t - 1))

        @pl.when(t > 1)
        def _():
            finish(mine(t - 1), other(t - 2))

    last = jnp.int32(na - 1)
    pass_block(last, False)
    multiply(other(last))
    finish(row)
    finish(mine(last), other(last - 1))
    finish(other(last))

    @pl.loop(0, na)
    def _(t):
        for own in (True, False):
            j = mine(t) if own else other(t)
            for h in range(PIECES):
                each_hop(t, own, h, lambda way: hop(panel.at[j, h], j, h, way).wait_send())
            for k in range(1, n_col):
                part_copy(j, k).wait_send()


def fused(dims, amplitudes, integrals, slot_tiles, tile_count, denominator):
    n_row, n_col, na, nb = dims
    tile_rows, tile_size, width = integrals.shape
    depth, pairs = amplitudes.shape
    groups = width // LANES
    rows = tile_rows * tile_size
    dma = pltpu.SemaphoreType.DMA
    return pl.pallas_call(
        functools.partial(kernel, dims),
        out_shape=jax.ShapeDtypeStruct(denominator.shape, jnp.bfloat16),
        in_specs=[pl.BlockSpec(memory_space=pltpu.VMEM)] * 2 + [pl.BlockSpec(memory_space=pl.ANY)] * 3,
        out_specs=pl.BlockSpec(memory_space=pltpu.VMEM),
        scratch_shapes=[
            pltpu.VMEM((n_row, PIECES, depth // PIECES, pairs), jnp.bfloat16),
            pltpu.VMEM((2 * groups * tile_rows + 1, tile_size, LANES), jnp.bfloat16),
            pltpu.VMEM((rows, depth), jnp.bfloat16),
            pltpu.VMEM((n_row, rows, pairs), jnp.bfloat16),
            pltpu.VMEM((n_col - 1, n_row, rows // n_col, pairs), jnp.bfloat16),
            pltpu.VMEM(denominator.shape, jnp.float32),
            pltpu.VMEM((tile_rows, -(-depth // tile_size // LANES) * LANES), jnp.int32),
            pltpu.SMEM((tile_rows, -(-depth // tile_size // LANES) * LANES), jnp.int32),
            dma((2 + PIECES,)),
            dma((groups,)),
            dma((n_row, PIECES, 3)),
            dma((n_row, PIECES)),
            dma((n_row, n_col - 1)),
            dma((n_row, n_col - 1)),
        ],
        compiler_params=pltpu.CompilerParams(
            collective_id=0, has_side_effects=True, vmem_limit_bytes=60 * 1024 * 1024
        ),
        name="ladder",
    )(slot_tiles, tile_count, amplitudes, integrals, denominator)


def spread_weights(weights, slot_ids, live_count, block_tiles):
    tile_rows, tile_size, _ = weights.shape
    slot_total = slot_ids.shape[1]
    offsets = jnp.arange(slot_total, dtype=jnp.int32)
    live_mask = offsets[None, :] < live_count
    tile_ids = jnp.arange(block_tiles, dtype=jnp.int32)
    selector = ((slot_ids[:, :, None] == tile_ids[None, None, :]) & live_mask[:, :, None]).astype(
        jnp.bfloat16
    )
    shaped = weights.reshape(tile_rows, tile_size, slot_total, tile_size)
    spread = jnp.einsum(
        "nxsk,nsg->nxgk", shaped, selector, preferred_element_type=jnp.float32
    ).astype(jnp.bfloat16)
    return spread.reshape(tile_rows * tile_size, block_tiles * tile_size)


def plain(amplitudes, integrals, slot_tiles, tile_count, denominator):
    block_tiles = amplitudes.shape[0] // integrals.shape[1]
    dense = spread_weights(integrals, slot_tiles, tile_count, block_tiles)
    panel = lax.all_gather(amplitudes, "row", axis=1, tiled=True)
    residual = lax.psum_scatter(
        jnp.dot(dense, panel, preferred_element_type=jnp.float32).astype(jnp.bfloat16),
        "col",
        scatter_dimension=0,
        tiled=True,
    ).astype(jnp.float32)
    return (residual / denominator).astype(jnp.bfloat16)


def shards(n_row, n_col, amplitudes, *rest):
    nb = 2
    if amplitudes.shape[1] % LANES == 0 and n_row % nb == 0:
        return fused((n_row, n_col, n_row // nb, nb), amplitudes, *rest)
    return plain(amplitudes, *rest)


def solution(mesh):
    return jax.shard_map(
        functools.partial(shards, mesh.shape["row"], mesh.shape["col"]),
        mesh=mesh,
        in_specs=(
            P("col", "row"),
            P("row", None, "col"),
            P("row", "col"),
            P("row", "col"),
            P(("row", "col"), None),
        ),
        out_specs=P(("row", "col"), None),
        check_vma=False,
    )
```

profile of v0, /device:TPU:0, one launch (start us, length us, event | category | flops | bytes accessed | tf_op | source)
XLA Modules:
  0.0 99.2 jit_solution(5871203584497061294)
XLA Ops:
  0.0 1.3 %copy.6.count_ref = s32[32,1]{1,0:T(8,128)} copy(s32[32,1]{0,1:T(1,128)} %param.8) | data formatting | bytes 256 | tf_op args[3]
  1.3 95.6 %ladder.1 = bf16[512,1024]{1,0:T(8,128)(2,1)} custom-call(s32[32,32]{1,0:T(8,128)} %slots_ref.1, s32[32,1]{1,0:T(8,128)} %copy.6.count_ref, bf16[4096,128]{1,0:T(8,128)(2,1)} %amp_ref.1, bf16[32,64,2048]{2,1,0:T(8,128)(2,1)} %ints_ref.1, f32[512,1024]{1,0:T(8,128)} %den_ref.1), custom_call_target="tpu_custom_call" | custom-call | tf_op jit(solution)/shard_map/ladder/pallas_call | solution.py:241
  97.0 2.3 %copy.8 = bf16[512,1024]{1,0:T(8,128)(2,1)} copy(bf16[512,1024]{1,0:T(8,128)(2,1)} %ladder.1) | data formatting | bytes 2097152
where the time goes:
time: 99.6 us; the launch traced here: 99.2 us
  Pallas kernels  95.6 us (96%)
  local copies, waits for them, and re-layouts  3.6 us (4%)
    pallas_call x1, Pallas kernels, fused(): pl.pallas_call(functools.partial(kernel, dims), out_shape=jax.ShapeDtypeS...  95.6 us
    unnamed x2, local copies, waits for them, and re-layouts  3.6 us

commit v1 on v0

--- a/solution.py
+++ b/solution.py
@@ -17,7 +17,7 @@
 
 def kernel(
     dims, slots_ref, count_ref, amp_ref, ints_ref, den_ref, out_ref,
-    panel, tiles, dense, partial, landed, den, table, table_ref,
+    panel, tiles, dense, partial, landed, den, slots_in, count_in, table, table_ref,
     load_sem, ints_sem, send_sem, recv_sem, part_send_sem, part_recv_sem,
 ):
     n_row, n_col, na, nb = dims
@@ -98,6 +98,10 @@
         pltpu.make_async_copy(amp_ref.at[piece(h)], panel.at[row, h], load_sem.at[1 + h]) for h in range(PIECES)
     ]
     load_den = pltpu.make_async_copy(den_ref, den, load_sem.at[0])
+    load_small = [
+        pltpu.make_async_copy(slots_ref, slots_in, load_sem.at[2 + PIECES]),
+        pltpu.make_async_copy(count_ref, count_in, load_sem.at[3 + PIECES]),
+    ]
 
     def load_ints(p):
         return pltpu.make_async_copy(
@@ -106,15 +110,22 @@
             ints_sem.at[p],
         )
 
+    for copy in load_small:
+        copy.start()
     for p in range(groups):
         load_ints(p).start()
     for copy in load_own:
         copy.start()
     load_den.start()
+    for copy in load_small:
+        copy.wait()
 
     virtual = lax.broadcasted_iota(jnp.int32, table.shape, 1)
     residual = lax.broadcasted_iota(jnp.int32, table.shape, 0)
-    slots, count = slots_ref[...], count_ref[...]
+    slots = slots_in[...]
+    square = (tile_rows, tile_rows)
+    diagonal = lax.broadcasted_iota(jnp.int32, square, 0) == lax.broadcasted_iota(jnp.int32, square, 1)
+    count = jnp.sum(jnp.where(diagonal, count_in[...], 0), axis=1, keepdims=True)
     found = jnp.full(table.shape, 2 * groups * tile_rows, jnp.int32)
     for s in range(slots.shape[1]):
         turned = jnp.where(virtual % 2 != s % 2, groups * tile_rows, 0)
@@ -240,8 +251,8 @@
     dma = pltpu.SemaphoreType.DMA
     return pl.pallas_call(
         functools.partial(kernel, dims),
-        out_shape=jax.ShapeDtypeStruct(denominator.shape, jnp.bfloat16),
-        in_specs=[pl.BlockSpec(memory_space=pltpu.VMEM)] * 2 + [pl.BlockSpec(memory_space=pl.ANY)] * 3,
+        out_shape=pltpu.VMEM(denominator.shape, jnp.bfloat16),
+        in_specs=[pl.BlockSpec(memory_space=pl.ANY)] * 5,
         out_specs=pl.BlockSpec(memory_space=pltpu.VMEM),
         scratch_shapes=[
             pltpu.VMEM((n_row, PIECES, depth // PIECES, pairs), jnp.bfloat16),
@@ -250,9 +261,11 @@
             pltpu.VMEM((n_row, rows, pairs), jnp.bfloat16),
             pltpu.VMEM((n_col - 1, n_row, rows // n_col, pairs), jnp.bfloat16),
             pltpu.VMEM(denominator.shape, jnp.float32),
+            pltpu.VMEM(slot_tiles.shape, jnp.int32),
+            pltpu.VMEM((1, tile_rows), jnp.int32),
             pltpu.VMEM((tile_rows, -(-depth // tile_size // LANES) * LANES), jnp.int32),
             pltpu.SMEM((tile_rows, -(-depth // tile_size // LANES) * LANES), jnp.int32),
-            dma((2 + PIECES,)),
+            dma((4 + PIECES,)),
             dma((groups,)),
             dma((n_row, PIECES, 3)),
             dma((n_row, PIECES)),
@@ -260,10 +273,10 @@
             dma((n_row, n_col - 1)),
         ],
         compiler_params=pltpu.CompilerParams(
-            collective_id=0, has_side_effects=True, vmem_limit_bytes=60 * 1024 * 1024
+            collective_id=0, has_side_effects=True, vmem_limit_bytes=58 * 1024 * 1024
         ),
         name="ladder",
-    )(slot_tiles, tile_count, amplitudes, integrals, denominator)
+    )(slot_tiles, tile_count.reshape(1, -1), amplitudes, integrals, denominator)
 
 
 def spread_weights(weights, slot_ids, live_count, block_tiles):

time: 99.6 us -> 95 us (0.954)
  local copies, waits for them, and re-layouts: 3.6 us -> 0.97 us
  Pallas kernels: 95.6 us -> 93.9 us
    unnamed x2 -> x1, local copies, waits for them, and re-layouts: 3.6 us -> 0.97 us
    pallas_call x1, Pallas kernels: 95.6 us -> 93.9 us  [fused(): pl.pallas_call(functools.partial(kernel, dims), out_shape=pltpu.VMEM(deno...]
where the time goes in v1:
time: 95 us; the launch traced here: 94.9 us
  Pallas kernels  93.9 us (99%)
  local copies, waits for them, and re-layouts  0.97 us (1%)
    pallas_call x1, Pallas kernels, fused(): pl.pallas_call(functools.partial(kernel, dims), out_shape=pltpu.VMEM(deno...  93.9 us

profile of v1, /device:TPU:0, one launch (start us, length us, event | category | flops | bytes accessed | tf_op | source)
XLA Modules:
  0.0 94.9 jit_solution(12227257843353156469)
XLA Ops:
  0.0 93.9 %ladder.1 = bf16[512,1024]{1,0:T(8,128)(2,1)S(1)} custom-call(s32[32,32]{1,0:T(8,128)} %slots_ref.1, s32[1,32]{1,0:T(1,128)} %bitcast.1, bf16[4096,128]{1,0:T(8,128)(2,1)} %amp_ref.1, bf16[32,64,2048]{2,1,0:T(8,128)(2,1)} %ints_ref.1, f32[512,1024]{1,0:T(8,128)} %den_ref.1), custom_call_target="tpu_custom_call" | custom-call | tf_op jit(solution)/shard_map/ladder/pallas_call | solution.py:252
  93.9 1.0 %copy.7 = bf16[512,1024]{1,0:T(8,128)(2,1)} copy(bf16[512,1024]{1,0:T(8,128)(2,1)S(1)} %ladder.1) | data formatting | bytes 2097152

commit v2 on v1

--- a/solution.py
+++ b/solution.py
@@ -9,6 +9,12 @@
 
 LANES = 128
 PIECES = 2
+SHARES = (1, 1)
+
+
+def cuts(depth):
+    unit = depth // sum(SHARES)
+    return [(sum(SHARES[:h]) * unit, SHARES[h] * unit) for h in range(PIECES)]
 
 
 def line_order(size, at):
@@ -18,7 +24,7 @@
 def kernel(
     dims, slots_ref, count_ref, amp_ref, ints_ref, den_ref, out_ref,
     panel, tiles, dense, partial, landed, den, slots_in, count_in, table, table_ref,
-    load_sem, ints_sem, send_sem, recv_sem, part_send_sem, part_recv_sem,
+    load_sem, ints_sem, send_sem, recv_sem, part_send_sem, part_recv_sem, ready_sem,
 ):
     n_row, n_col, na, nb = dims
     tile_rows = ints_ref.shape[0]
@@ -47,8 +53,10 @@
 
     pl.semaphore_signal(barrier, inc=1, device_id=across)
     for k in range(1, n_col):
-        pl.semaphore_signal(barrier, inc=1, device_id={"col": lax.rem(col + k, n_col)})
-    pl.semaphore_wait(barrier, n_col + has_up.astype(jnp.int32) + has_down.astype(jnp.int32))
+        pl.when(col < k)(lambda: pl.semaphore_signal(barrier, inc=1, device_id={"col": k}))
+    pl.semaphore_wait(barrier, 1 + col + has_up.astype(jnp.int32) + has_down.astype(jnp.int32))
+    for k in range(n_col - 1):
+        pl.when(col > k)(lambda: pl.semaphore_signal(ready_sem, inc=1, device_id={"col": k}))
 
     def order(t):
         value = jnp.int32(0)
@@ -63,39 +71,45 @@
     def other(t):
         return order(t) * nb + 1 - side
 
+    parts = cuts(depth)
+    inside = has_up & has_down
+
+    def piece(h):
+        return pl.ds(*parts[h])
+
     def hop(source, j, h, way):
         to = (up, down, across)[way]
         return pltpu.make_async_remote_copy(
-            source, panel.at[j, h], send_sem.at[j, h, way], recv_sem.at[j, h], device_id=to
+            source.at[piece(h)], panel.at[j, piece(h)], send_sem.at[j, h, way], recv_sem.at[j, h], device_id=to
         )
 
-    def each_hop(t, own, h, act):
+    def each_hop(t, own, h, source, j, act):
+        def go(way):
+            act(hop(source, j, h, way))
+
         a = order(t)
         goes_up, goes_down = has_up & (a <= pos), has_down & (a >= pos)
         if not own and h < PIECES // 2:
             return
         if not own:
             goes_up, goes_down = goes_up & (a == 0), goes_down & (a == na - 1)
-        pl.when(goes_up)(lambda: act(0))
-        pl.when(goes_down)(lambda: act(1))
+        pl.when(goes_up)(lambda: go(0))
+        pl.when(goes_down)(lambda: go(1))
         if own and h < PIECES // 2:
-            act(2)
+            go(2)
         elif own:
-            pl.when((a == pos) | ((a > 0) & (a < na - 1)))(lambda: act(2))
-
-    def piece(h):
-        return pl.ds(h * (depth // PIECES), depth // PIECES)
+            pl.when((a == pos) | ((a > 0) & (a < na - 1)))(lambda: go(2))
 
     def pass_on(t, own, h):
         j = mine(t) if own else other(t)
-        hop(panel.at[j, h], j, h, 2).wait_recv()
-        each_hop(t, own, h, lambda way: hop(panel.at[j, h], j, h, way).start())
+        hop(panel.at[j], j, h, 2).wait_recv()
+        each_hop(t, own, h, panel.at[j], j, lambda copy: copy.start())
 
     for h in range(PIECES):
-        each_hop(jnp.int32(0), True, h, lambda way: hop(amp_ref.at[piece(h)], row, h, way).start())
+        each_hop(jnp.int32(0), True, h, amp_ref, row, lambda copy: copy.start())
 
     load_own = [
-        pltpu.make_async_copy(amp_ref.at[piece(h)], panel.at[row, h], load_sem.at[1 + h]) for h in range(PIECES)
+        pltpu.make_async_copy(amp_ref.at[piece(h)], panel.at[row, piece(h)], load_sem.at[1 + h]) for h in range(PIECES)
     ]
     load_den = pltpu.make_async_copy(den_ref, den, load_sem.at[0])
     load_small = [
@@ -162,53 +176,53 @@
         copy.wait()
     load_den.wait()
 
-    def target(k):
-        chip = lax.rem(col // 2 + k // 2, n_col // 2)
-        return chip * 2 + lax.rem(col + k, 2)
-
-    def rows_of(k):
-        return pl.ds(pl.multiple_of(target(k) * quarter, quarter), quarter)
-
-    def part_copy(j, k):
+    chips, chip, core = n_col // 2, col // 2, lax.rem(col, 2)
+
+    def target(i):
+        return lax.rem(chip + i // 2 + 1, chips) * 2 + lax.rem(core + 1 + i, 2)
+
+    def rows_of(i):
+        return pl.ds(pl.multiple_of(target(i) * quarter, quarter), quarter)
+
+    def part_copy(j, i):
         return pltpu.make_async_remote_copy(
-            partial.at[j, rows_of(k)], landed.at[k - 1, j],
-            part_send_sem.at[j, k - 1], part_recv_sem.at[j, k - 1], device_id={"col": target(k)},
+            partial.at[j, rows_of(i)], landed.at[i, j],
+            part_send_sem.at[j, i], part_recv_sem.at[j, i], device_id={"col": target(i)},
         )
+
+    def hand_out(i, *blocks):
+        @pl.when(i < n_col - 1)
+        def _():
+            for j in blocks:
+                part_copy(j, i).start()
 
     def multiply(*blocks):
         @pl.loop(0, n_col)
         def _(i):
-            k = n_col - 1 - i
-            rows = rows_of(k)
-            right = [panel[j].reshape(depth, pairs) for j in blocks]
+            rows = rows_of(i)
+            right = [panel[j] for j in blocks]
             right = right[0] if len(right) == 1 else jnp.concatenate(right, axis=1)
             product = jnp.dot(dense[rows, :], right, preferred_element_type=jnp.float32).astype(jnp.bfloat16)
             for n, j in enumerate(blocks):
                 partial[j, rows, :] = product[:, n * pairs:(n + 1) * pairs]
-
-            @pl.when(k > 0)
-            def _():
-                for j in blocks:
-                    part_copy(j, k).start()
-
-    def finish(*blocks):
-        for j in blocks:
-            for k in range(1, n_col):
-                part_copy(j, k).wait_recv()
-            total = partial[j, rows_of(0), :].astype(jnp.float32)
-            for k in range(1, n_col):
-                total = total + landed[k - 1, j].astype(jnp.float32)
-            columns = pl.ds(pl.multiple_of(j * pairs, pairs), pairs)
-            out_ref[:, columns] = (total / den[:, columns]).astype(jnp.bfloat16)
+            hand_out(i, *blocks)
+
+    def finish(j):
+        total = partial[j, rows_of(n_col - 1), :].astype(jnp.float32)
+        for i in range(n_col - 2, -1, -1):
+            part_copy(j, i).wait_recv()
+            total = total + landed[i, j].astype(jnp.float32)
+        columns = pl.ds(pl.multiple_of(j * pairs, pairs), pairs)
+        out_ref[:, columns] = (total / den[:, columns]).astype(jnp.bfloat16)
 
     def pass_block(t, own):
         for h in reversed(range(PIECES)) if not own else range(PIECES):
             pass_on(t, own, h)
 
-    inside = has_up & has_down
     pass_block(jnp.int32(1), True)
     pl.when(inside)(lambda: pass_block(jnp.int32(2), True))
     pass_block(jnp.int32(0), False)
+    pl.when(col < n_col - 1)(lambda: pl.semaphore_wait(ready_sem, n_col - 1 - col))
     multiply(row)
 
     @pl.loop(1, na)
@@ -221,25 +235,40 @@
 
         multiply(mine(t), other(t - 1))
 
-        @pl.when(t > 1)
+        @pl.when(t == 1)
         def _():
-            finish(mine(t - 1), other(t - 2))
+            finish(row)
+
+        @pl.when((t > 1) & (t < na - 1))
+        def _():
+            finish(mine(t - 1))
+            finish(other(t - 2))
 
     last = jnp.int32(na - 1)
     pass_block(last, False)
     multiply(other(last))
-    finish(row)
-    finish(mine(last), other(last - 1))
-    finish(other(last))
+    def sent(j):
+        for i in range(n_col - 1):
+            part_copy(j, i).wait_send()
 
     @pl.loop(0, na)
     def _(t):
         for own in (True, False):
             j = mine(t) if own else other(t)
             for h in range(PIECES):
-                each_hop(t, own, h, lambda way: hop(panel.at[j, h], j, h, way).wait_send())
-            for k in range(1, n_col):
-                part_copy(j, k).wait_send()
+                each_hop(t, own, h, panel.at[j], j, lambda copy: copy.wait_send())
+            if own:
+                sent(j)
+            else:
+                pl.when(t < na - 1)(lambda: sent(j))
+
+    if na > 2:
+        finish(mine(last - 1))
+        finish(other(last - 2))
+    finish(mine(last))
+    finish(other(last - 1))
+    finish(other(last))
+    sent(other(last))
 
 
 def fused(dims, amplitudes, integrals, slot_tiles, tile_count, denominator):
@@ -255,7 +284,7 @@
         in_specs=[pl.BlockSpec(memory_space=pl.ANY)] * 5,
         out_specs=pl.BlockSpec(memory_space=pltpu.VMEM),
         scratch_shapes=[
-            pltpu.VMEM((n_row, PIECES, depth // PIECES, pairs), jnp.bfloat16),
+            pltpu.VMEM((n_row, depth, pairs), jnp.bfloat16),
             pltpu.VMEM((2 * groups * tile_rows + 1, tile_size, LANES), jnp.bfloat16),
             pltpu.VMEM((rows, depth), jnp.bfloat16),
             pltpu.VMEM((n_row, rows, pairs), jnp.bfloat16),
@@ -271,6 +300,7 @@
             dma((n_row, PIECES)),
             dma((n_row, n_col - 1)),
             dma((n_row, n_col - 1)),
+            pltpu.SemaphoreType.REGULAR,
         ],
         compiler_params=pltpu.CompilerParams(
             collective_id=0, has_side_effects=True, vmem_limit_bytes=58 * 1024 * 1024
@@ -310,7 +340,7 @@
 
 def shards(n_row, n_col, amplitudes, *rest):
     nb = 2
-    if amplitudes.shape[1] % LANES == 0 and n_row % nb == 0:
+    if amplitudes.shape[1] % LANES == 0 and n_row % nb == 0 and n_row > nb and n_col % 2 == 0 and amplitudes.shape[0] % (sum(SHARES) * LANES) == 0:
         return fused((n_row, n_col, n_row // nb, nb), amplitudes, *rest)
     return plain(amplitudes, *rest)
 

time: 95 us -> 94.9 us (level)
  no operation moved by 1% of the time
where the time goes in v2:
time: 94.9 us; the launch traced here: 94.7 us
  Pallas kernels  93.7 us (99%)
  local copies, waits for them, and re-layouts  0.97 us (1%)
    pallas_call x1, Pallas kernels, fused(): pl.pallas_call(functools.partial(kernel, dims), out_shape=pltpu.VMEM(deno...  93.7 us

profile of v2, /device:TPU:0, one launch (start us, length us, event | category | flops | bytes accessed | tf_op | source)
XLA Modules:
  0.0 94.7 jit_solution(3049958325724016427)
XLA Ops:
  0.0 93.7 %ladder.1 = bf16[512,1024]{1,0:T(8,128)(2,1)S(1)} custom-call(s32[32,32]{1,0:T(8,128)} %slots_ref.1, s32[1,32]{1,0:T(1,128)} %bitcast.1, bf16[4096,128]{1,0:T(8,128)(2,1)} %amp_ref.1, bf16[32,64,2048]{2,1,0:T(8,128)(2,1)} %ints_ref.1, f32[512,1024]{1,0:T(8,128)} %den_ref.1), custom_call_target="tpu_custom_call" | custom-call | tf_op jit(solution)/shard_map/ladder/pallas_call | solution.py:281
  93.8 1.0 %copy.7 = bf16[512,1024]{1,0:T(8,128)(2,1)} copy(bf16[512,1024]{1,0:T(8,128)(2,1)S(1)} %ladder.1) | data formatting | bytes 2097152
